TPU v7x, 32 devices: a whole 2x2x4 slice. The times are simulated.
32 devices in a mesh: gx: 4 (over y, core), gy: 8 (over z, x).
Axes of the slice: x: 2, y: 2, z: 4, core: 2. Of those that a mesh axis runs over, the one named last changes fastest.
Arguments:
- perturbation: float32 [5, 16, 512], P(None, 'gx', 'gy'), may hold values from -6 to 6
- mean_velocity: float32 [16, 512], P('gx', 'gy'), may hold values from 0.2 to 0.9
- mean_shear: float32 [16, 512], P('gx', 'gy'), may hold values from -4 to 4
- cotangent: float32 [5, 16, 512], P(None, 'gx', 'gy'), may hold values from -6 to 6
- kernel_in: bfloat16 [64, 135], replicated, may hold values from -0.5 to 0.5
- kernel_mid: bfloat16 [64, 1728], replicated, may hold values from -0.15625 to 0.15625
- kernel_out: bfloat16 [5, 1728], replicated, may hold values from -0.15625 to 0.15625
Outputs:
- advanced: float32 [5, 16, 512], P(None, 'gx', 'gy')
- grad_in: float32 [64, 135], replicated
- grad_mid: float32 [64, 1728], replicated
- grad_out: float32 [5, 1728], replicated
All inputs are finite; a program needn't handle non-finite values.
Results may differ from a plain program's by a relative error of at most 0.0065.
Values may be sent and summed in bfloat16 or wider, within the bound.
A program may use at most 64 MiB of HBM per device.

v0:
```python
import math
import jax
import jax.numpy as jnp
from jax import lax
from jax.sharding import PartitionSpec as P

NZ = 8
STEPS = 2
TIME_STEP = 0.25
STENCIL_WEIGHTS = (0.75, -0.15, 1.0 / 60.0)


def padded_2(cells, sides, width):
    for axis, dim in sides:
        count = lax.axis_size(axis)
        ends = count - 1
        head = lax.slice_in_dim(cells, 0, width, axis=dim)
        tail = lax.slice_in_dim(cells, cells.shape[dim] - width, cells.shape[dim], axis=dim)
        cells = jnp.concatenate(
            [
                lax.ppermute(tail, axis, [(i, (i + 1) % count) for i in range(ends)]),
                cells,
                lax.ppermute(head, axis, [((i + 1) % count, i) for i in range(ends)]),
            ],
            axis=dim,
        )
    return cells


def wrap_depth(grid_field, margin):
    size_z = grid_field.shape[3]
    return jnp.concatenate(
        [grid_field[:, :, :, size_z - margin :], grid_field, grid_field[:, :, :, :margin]], axis=3
    )


def difference(padded, direction, margin, length):
    summed = None
    for offset, weight in zip((1, 2, 3), STENCIL_WEIGHTS):
        upper_cells = lax.slice_in_dim(
            padded, margin + offset, margin + offset + length, axis=direction
        )
        lower_cells = lax.slice_in_dim(
            padded, margin - offset, margin - offset + length, axis=direction
        )
        contrib = weight * (upper_cells - lower_cells)
        summed = contrib if summed is None else summed + contrib
    return summed


def rates_from(padded, margin, velocity, shear_rate):
    size_x = padded.shape[1] - 2 * margin
    size_y = padded.shape[2] - 2 * margin
    interior = padded[:, margin : margin + size_x, margin : margin + size_y]
    slope_x = difference(padded[:, :, margin : margin + size_y], 1, margin, size_x)
    slope_y = difference(padded[:, margin : margin + size_x], 2, margin, size_y)
    slope_z = difference(wrap_depth(interior, 3), 3, 3, interior.shape[3])
    divergence = slope_x[1] + slope_y[2] + slope_z[3]
    return jnp.stack(
        [
            -velocity * slope_x[0] - divergence,
            -velocity * slope_x[1] - shear_rate * interior[2] - slope_x[4],
            -velocity * slope_x[2] - slope_y[4],
            -velocity * slope_x[3] - slope_z[4],
            -velocity * slope_x[4] - divergence,
        ]
    )


def adjoint_fields(adjoint_in, velocity):
    acoustic = adjoint_in[0] + adjoint_in[4]
    return jnp.stack(
        [
            velocity * adjoint_in[0],
            velocity * adjoint_in[1] + acoustic,
            velocity * adjoint_in[2],
            velocity * adjoint_in[3],
            velocity * adjoint_in[4] + adjoint_in[1],
            acoustic,
            adjoint_in[2],
            adjoint_in[3],
        ]
    )


def adjoint_from(padded, margin, adjoint_in, shear_rate):
    size_x = padded.shape[1] - 2 * margin
    size_y = padded.shape[2] - 2 * margin
    interior = padded[:, margin : margin + size_x, margin : margin + size_y]
    slope_x = difference(padded[:5, :, margin : margin + size_y], 1, margin, size_x)
    slope_y = difference(padded[5:, margin : margin + size_x], 2, margin, size_y)
    slope_z = difference(wrap_depth(interior[5:], 3), 3, 3, interior.shape[3])
    return jnp.stack(
        [
            slope_x[0],
            slope_x[1],
            slope_x[2] - shear_rate * adjoint_in[1] + slope_y[0],
            slope_x[3] + slope_z[0],
            slope_x[4] + slope_y[1] + slope_z[2],
        ]
    )


def conv_valid(padded, kernel):
    return lax.conv_general_dilated(
        padded[None],
        kernel,
        (1, 1, 1),
        "VALID",
        dimension_numbers=("NCDHW", "OIDHW", "NCDHW"),
        preferred_element_type=jnp.float32,
    )[0]


def flip_kernel(kernel):
    return jnp.transpose(jnp.flip(kernel, (2, 3, 4)), (1, 0, 2, 3, 4))


def kernel_grad(padded, gradient):
    channels = padded.shape[0]
    size_x, size_y, size_z = (gradient.shape[1], gradient.shape[2], gradient.shape[3])
    flat_grad = gradient.reshape(gradient.shape[0], -1)
    pieces = []
    for shift_x in range(3):
        for shift_y in range(3):
            for shift_z in range(3):
                window = padded[
                    :,
                    shift_x : shift_x + size_x,
                    shift_y : shift_y + size_y,
                    shift_z : shift_z + size_z,
                ]
                pieces.append(
                    lax.dot_general(
                        flat_grad,
                        window.reshape(channels, -1),
                        (((1,), (1,)), ((), ())),
                        preferred_element_type=jnp.float32,
                    )
                )
    stacked = jnp.stack(pieces)
    return jnp.transpose(stacked, (1, 2, 0)).reshape(gradient.shape[0], channels * 27)


def closure_backward(saved, source_grad, kernels, need_input, padding_fn):
    kernel_in, kernel_mid, kernel_out = kernels
    padded_in, hidden_one, padded_one, hidden_two, padded_two = saved
    error_out = source_grad.astype(jnp.bfloat16)
    grad_out = kernel_grad(padded_two, error_out)
    back_mid = conv_valid(padding_fn(error_out), flip_kernel(kernel_out)) * (
        1.0 - jnp.square(hidden_two.astype(jnp.float32))
    )
    error_mid = back_mid.astype(jnp.bfloat16)
    grad_mid = kernel_grad(padded_one, error_mid)
    back_in = conv_valid(padding_fn(error_mid), flip_kernel(kernel_mid)) * (
        1.0 - jnp.square(hidden_one.astype(jnp.float32))
    )
    error_in = back_in.astype(jnp.bfloat16)
    grad_in = kernel_grad(padded_in, error_in)
    state_grad = conv_valid(padding_fn(error_in), flip_kernel(kernel_in)) if need_input else None
    return ((grad_in, grad_mid, grad_out), state_grad)


def retreat(adjoint_in, adjoint_fn):
    into_second = 2.0 / 3.0 * adjoint_in + 2.0 / 3.0 * TIME_STEP * adjoint_fn(adjoint_in)
    direct = 1.0 / 3.0 * adjoint_in
    into_first = 0.25 * into_second + 0.25 * TIME_STEP * adjoint_fn(into_second)
    direct = direct + 0.75 * into_second
    carried = direct + into_first + TIME_STEP * adjoint_fn(into_first)
    source_grad = TIME_STEP * (2.0 / 3.0 * adjoint_in + 0.25 * into_second + into_first)
    return (carried, source_grad)


def grad_pad(grid_field):
    return wrap_depth(padded_2(grid_field, (("gx", 1), ("gy", 2)), 1), 1)


def inside(size_x, size_y, margin):
    start_x = lax.axis_index("gx") * size_x - margin
    start_y = lax.axis_index("gy") * size_y - margin
    index_x = start_x + jnp.arange(size_x + 2 * margin, dtype=jnp.int32)
    index_y = start_y + jnp.arange(size_y + 2 * margin, dtype=jnp.int32)
    valid_x = (index_x >= 0) & (index_x < size_x * lax.axis_size("gx"))
    valid_y = (index_y >= 0) & (index_y < size_y * lax.axis_size("gy"))
    return (valid_x[:, None] & valid_y[None, :]).astype(jnp.float32)[None, :, :, None]


def closure_deep(grid_field, kernels):
    kernel_in, kernel_mid, kernel_out = kernels
    size_x, size_y = (grid_field.shape[1], grid_field.shape[2])
    extended = padded_2(grid_field, (("gx", 1), ("gy", 2)), 3)
    input_wide = extended.astype(jnp.bfloat16)
    hidden_wide = (
        jnp.tanh(conv_valid(wrap_depth(input_wide, 1), kernel_in)) * inside(size_x, size_y, 2)
    ).astype(jnp.bfloat16)
    second_wide = (
        jnp.tanh(conv_valid(wrap_depth(hidden_wide, 1), kernel_mid)) * inside(size_x, size_y, 1)
    ).astype(jnp.bfloat16)
    source = conv_valid(wrap_depth(second_wide, 1), kernel_out)
    saved = (
        wrap_depth(input_wide[:, 2:-2, 2:-2], 1),
        hidden_wide[:, 2:-2, 2:-2],
        wrap_depth(hidden_wide[:, 1:-1, 1:-1], 1),
        second_wide[:, 1:-1, 1:-1],
        wrap_depth(second_wide, 1),
    )
    return (extended, source, saved)


def body(perturbation, mean_velocity, mean_shear, cotangent, kernel_in, kernel_mid, kernel_out):
    channels = perturbation.shape[0]
    hidden = kernel_in.shape[0]
    size_x = perturbation.shape[1]
    size_y = perturbation.shape[2] // NZ
    current = perturbation.reshape(channels, size_x, size_y, NZ)
    velocity = mean_velocity.reshape(size_x, size_y, NZ)
    shear_rate = mean_shear.reshape(size_x, size_y, NZ)
    kernels = (
        kernel_in.reshape(hidden, channels, 3, 3, 3),
        kernel_mid.reshape(hidden, hidden, 3, 3, 3),
        kernel_out.reshape(channels, hidden, 3, 3, 3),
    )

    def section_rates(grid_field):
        padded = padded_2(grid_field, (("gx", 1), ("gy", 2)), 3)
        return rates_from(padded, 3, velocity, shear_rate)

    def adjoint_rates(adjoint_in):
        padded = padded_2(adjoint_fields(adjoint_in, velocity), (("gx", 1), ("gy", 2)), 3)
        return adjoint_from(padded, 3, adjoint_in, shear_rate)

    def evaluate(grid_field, with_rates):
        extended, source, saved = closure_deep(grid_field, kernels)
        rate_field = rates_from(extended, 3, velocity, shear_rate) if with_rates else None
        return (source, saved, rate_field)

    history = []
    stored = []
    for step_index in range(STEPS):
        source, saved, rate_field = evaluate(current, True)
        history.append(current)
        stored.append(saved)
        section_one = current + TIME_STEP * (rate_field + source)
        section_two = 0.75 * current + 0.25 * (
            section_one + TIME_STEP * (section_rates(section_one) + source)
        )
        current = 1.0 / 3.0 * current + 2.0 / 3.0 * (
            section_two + TIME_STEP * (section_rates(section_two) + source)
        )
    cell_count = size_x * lax.axis_size("gx") * size_y * lax.axis_size("gy") * NZ
    adjoint_in = cotangent.reshape(channels, size_x, size_y, NZ) * (1.0 / math.sqrt(cell_count))
    totals = None
    for step_index in reversed(range(STEPS)):
        carried, source_grad = retreat(adjoint_in, adjoint_rates)
        saved = evaluate(history[step_index], False)[1]
        kernel_grads, state_grad = closure_backward(
            saved, source_grad, kernels, step_index > 0, grad_pad
        )
        totals = (
            kernel_grads
            if totals is None
            else tuple((sum_old + sum_new for sum_old, sum_new in zip(totals, kernel_grads)))
        )
        if step_index > 0:
            adjoint_in = carried + state_grad
    result = lax.psum((totals[0], totals[1], totals[2]), ("gx", "gy"))
    return (current.reshape(channels, size_x, size_y * NZ), result[0], result[1], result[2])


def solution(mesh):
    return jax.shard_map(
        body,
        mesh=mesh,
        in_specs=(
            P(None, "gx", "gy"),
            P("gx", "gy"),
            P("gx", "gy"),
            P(None, "gx", "gy"),
            P(),
            P(),
            P(),
        ),
        out_specs=(P(None, "gx", "gy"), P(), P(), P()),
        check_vma=False,
    )
```

profile of v0, /device:TPU:0, one launch (start us, length us, event | category | flops | bytes accessed | tf_op | source)
XLA Modules:
  0.0 642.7 jit_solution(11449475301091532205)
XLA Ops:
  8.0 2.4 collective-permute-start.1
  14.4 5.8 collective-permute-start.25
  24.3 1.9 copy.1395
  30.3 3.4 collective-permute-start.3
  33.7 1.3 collective-permute-start.2
  35.9 5.2 collective-permute-start.27
  44.1 2.1 copy.1387
  46.2 2.5 convolution_tanh_fusion
  50.0 5.2 fusion.164
  58.3 2.8 fusion.175
  64.0 1.7 collective-permute-start.28
  65.7 3.4 collective-permute-start.29
  70.2 4.3 collective-permute-start.31
  75.9 1.7 collective-permute-done.31
  77.6 5.0 collective-permute-done.30
  85.2 3.2 collective-permute-start.5
  92.4 7.0 %collective-permute-start.32 = (bf16[5,1,8,8]{3,2,1,0:T(8,128)(2,1)S(1)}, bf16[5,1,8,8]{3,2,1,0:T(8,128)(2,1)S(1)}, u32[]{:S(2)}, u32[]{:S(2)}) collective-permute-start(bf16[5,1,8,8]{3,2,1,0:T(8,128)(2,1)S(1)} %get-tuple-element.302), channel_id=1, source_target_pairs={{0,8},{8,16},{16,24},{1,9},{9,17},{17,25},{2,10},{10,18},{18,26},{... | collective-permute-start | bytes 1928 | tf_op jit(solution)/shard_map/ppermute | solution.py:21
  101.6 5.4 collective-permute-start.34
  107.7 3.3 collective-permute-start.41
  112.3 1.4 fusion.898
  113.8 4.5 collective-permute-start.7
  118.4 1.3 collective-permute-start.6
  120.1 4.6 collective-permute-start.43
  124.7 1.3 collective-permute-start.42
  126.4 3.9 collective-permute-start.9
  130.3 1.3 collective-permute-start.8
  132.1 1.8 collective-permute-done.8
  133.9 5.4 collective-permute-start.11
  141.6 5.2 collective-permute-done.10
  147.8 3.7 collective-permute-start.13
  153.2 2.0 collective-permute-done.12
  155.3 4.8 collective-permute-start.15
  162.4 4.3 collective-permute-done.14
  168.9 1.9 copy.1400
  170.8 2.5 fusion.691
  174.6 5.2 fusion.162
  181.3 4.2 collective-permute-start.36
  186.6 2.8 fusion.173
  206.7 4.5 collective-permute-start.38
  215.4 3.7 collective-permute-start.44
  232.7 5.0 collective-permute-start.46
  239.0 2.8 fusion.171
  244.2 3.7 collective-permute-start.49
  249.0 4.5 collective-permute-start.51
  254.9 1.7 collective-permute-done.51
  256.6 5.3 collective-permute-done.50
  265.2 3.6 collective-permute-start.53
  269.0 5.0 collective-permute-start.17
  277.2 4.8 collective-permute-start.19
  283.7 5.2 collective-permute-start.55
  291.5 5.4 collective-permute-done.54
  299.9 2.8 collective-permute-start.21
  305.6 4.4 collective-permute-start.56
  319.4 4.5 collective-permute-start.58
  326.7 1.4 fusion.899
  329.5 3.5 collective-permute-start.60
  340.2 4.7 collective-permute-start.62
  371.5 4.9 collective-permute-start.23
  378.1 1.6 collective-permute-done.23
  379.7 5.2 collective-permute-done.22
  386.8 111.3 %all-reduce.6.cloned.1.call-done = (f32[64,135]{0,1:T(8,128)}, f32[5,1728]{1,0:T(8,128)}) async-done(((f32[64,135]{0,1:T(8,128)}, f32[5,1728]{1,0:T(8,128)}), (f32[64,135]{0,1:T(8,128)}, f32[5,1728]{1,0:T(8,128)})) %all-reduce.6.cloned.1.call-update) | async-done | bytes 69136 | tf_op jit(solution)/shard_map/psum | solution.py:266
  498.1 1.6 copy.1540
  499.7 133.0 %all-reduce.4.cloned.1.call-done = f32[64,1728]{0,1:T(8,128)} async-done(((f32[64,1728]{0,1:T(8,128)}), f32[64,1728]{0,1:T(8,128)}) %all-reduce.4.cloned.1.call-update) | async-done | bytes 442384 | tf_op jit(solution)/shard_map/psum | solution.py:266
  632.7 2.2 copy.1541
  (783 shorter events, 158.4 us)
Async XLA Ops:
  7.2 491.0 %all-reduce.6.cloned.1.call-start = ((), (), s32[]{:S(2)}) async-start(), calls=%async_computation.1 | async-start | bytes 253952 | tf_op jit(solution)/shard_map/psum | solution.py:266
  8.0 21.2 %collective-permute-start.1 = (f32[5,3,8,8]{3,2,1,0:T(8,128)S(1)}, f32[5,3,8,8]{3,2,1,0:T(8,128)S(1)}, u32[]{:S(2)}, u32[]{:S(2)}) collective-permute-start(f32[5,3,8,8]{3,2,1,0:T(8,128)S(1)} %get-tuple-element.273), channel_id=1, source_target_pairs={{0,8},{8,16},{16,24},{1,9},{9,17},{17,25},{2,10},{10,18},{18,26},{... | collective-permute-start | bytes 11528 | tf_op jit(solution)/shard_map/ppermute | solution.py:21
  10.5 19.8 %collective-permute-start = (f32[5,3,8,8]{3,2,1,0:T(8,128)S(1)}, f32[5,3,8,8]{3,2,1,0:T(8,128)S(1)}, u32[]{:S(2)}, u32[]{:S(2)}) collective-permute-start(f32[5,3,8,8]{3,2,1,0:T(8,128)S(1)} %get-tuple-element.272), channel_id=1, source_target_pairs={{8,0},{16,8},{24,16},{9,1},{17,9},{25,17},{10,2},{18,10},{26,18},{... | collective-permute-start | bytes 11528 | tf_op jit(solution)/shard_map/ppermute | solution.py:23
  13.1 21.9 %collective-permute-start.24 = (f32[8,3,8,8]{3,2,1,0:T(8,128)S(1)}, f32[8,3,8,8]{3,2,1,0:T(8,128)S(1)}, u32[]{:S(2)}, u32[]{:S(2)}) collective-permute-start(f32[8,3,8,8]{3,2,1,0:T(8,128)S(1)} %get-tuple-element.202), channel_id=1, source_target_pairs={{8,0},{16,8},{24,16},{9,1},{17,9},{25,17},{10,2},{18,10},{26,18},{... | collective-permute-start | bytes 18440 | tf_op jit(solution)/shard_map/ppermute | solution.py:23
  14.4 20.6 %collective-permute-start.25 = (f32[8,3,8,8]{3,2,1,0:T(8,128)S(1)}, f32[8,3,8,8]{3,2,1,0:T(8,128)S(1)}, u32[]{:S(2)}, u32[]{:S(2)}) collective-permute-start(f32[8,3,8,8]{3,2,1,0:T(8,128)S(1)} %get-tuple-element.201), channel_id=1, source_target_pairs={{0,8},{8,16},{16,24},{1,9},{9,17},{17,25},{2,10},{10,18},{18,26},{... | collective-permute-start | bytes 18440 | tf_op jit(solution)/shard_map/ppermute | solution.py:21
  30.3 12.2 %collective-permute-start.3 = (f32[5,10,3,8]{3,2,1,0:T(4,128)S(1)}, f32[5,10,3,8]{3,2,1,0:T(4,128)S(1)}, u32[]{:S(2)}, u32[]{:S(2)}) collective-permute-start(f32[5,10,3,8]{3,2,1,0:T(4,128)S(1)} %get-tuple-element.153), channel_id=1, source_target_pairs={{0,1},{1,2},{2,3},{3,4},{4,5},{5,6},{6,7},{8,9},{9,10},{10,11},{11... | collective-permute-start | bytes 14408 | tf_op jit(solution)/shard_map/ppermute | solution.py:21
  33.7 8.7 %collective-permute-start.2 = (f32[5,10,3,8]{3,2,1,0:T(4,128)S(1)}, f32[5,10,3,8]{3,2,1,0:T(4,128)S(1)}, u32[]{:S(2)}, u32[]{:S(2)}) collective-permute-start(f32[5,10,3,8]{3,2,1,0:T(4,128)S(1)} %get-tuple-element.152), channel_id=1, source_target_pairs={{1,0},{2,1},{3,2},{4,3},{5,4},{6,5},{7,6},{9,8},{10,9},{11,10},{12... | collective-permute-start | bytes 14408 | tf_op jit(solution)/shard_map/ppermute | solution.py:23
  35.9 27.0 %collective-permute-start.27 = (f32[8,10,3,8]{3,2,1,0:T(4,128)}, f32[8,10,3,8]{3,2,1,0:T(4,128)}, u32[]{:S(2)}, u32[]{:S(2)}) collective-permute-start(f32[8,10,3,8]{3,2,1,0:T(4,128)} %get-tuple-element.95), channel_id=1, source_target_pairs={{0,1},{1,2},{2,3},{3,4},{4,5},{5,6},{6,7},{8,9},{9,10},{10,11},{11... | collective-permute-start | bytes 23048 | tf_op jit(solution)/shard_map/ppermute | solution.py:21
  41.1 21.8 %collective-permute-start.26 = (f32[8,10,3,8]{3,2,1,0:T(4,128)}, f32[8,10,3,8]{3,2,1,0:T(4,128)}, u32[]{:S(2)}, u32[]{:S(2)}) collective-permute-start(f32[8,10,3,8]{3,2,1,0:T(4,128)} %get-tuple-element.94), channel_id=1, source_target_pairs={{1,0},{2,1},{3,2},{4,3},{5,4},{6,5},{7,6},{9,8},{10,9},{11,10},{12... | collective-permute-start | bytes 23048 | tf_op jit(solution)/shard_map/ppermute | solution.py:23
  64.0 5.4 collective-permute-start.28
  65.7 4.4 collective-permute-start.29
  70.2 7.4 %collective-permute-start.31 = (f32[8,10,3,8]{3,2,1,0:T(4,128)S(1)}, f32[8,10,3,8]{3,2,1,0:T(4,128)S(1)}, u32[]{:S(2)}, u32[]{:S(2)}) collective-permute-start(f32[8,10,3,8]{3,2,1,0:T(4,128)S(1)} %get-tuple-element.93), channel_id=1, source_target_pairs={{0,1},{1,2},{2,3},{3,4},{4,5},{5,6},{6,7},{8,9},{9,10},{10,11},{11... | collective-permute-start | bytes 23048 | tf_op jit(solution)/shard_map/ppermute | solution.py:21
  74.5 8.1 %collective-permute-start.30 = (f32[8,10,3,8]{3,2,1,0:T(4,128)S(1)}, f32[8,10,3,8]{3,2,1,0:T(4,128)S(1)}, u32[]{:S(2)}, u32[]{:S(2)}) collective-permute-start(f32[8,10,3,8]{3,2,1,0:T(4,128)S(1)} %get-tuple-element.92), channel_id=1, source_target_pairs={{1,0},{2,1},{3,2},{4,3},{5,4},{6,5},{7,6},{9,8},{10,9},{11,10},{12... | collective-permute-start | bytes 23048 | tf_op jit(solution)/shard_map/ppermute | solution.py:23
  85.2 28.6 %collective-permute-start.5 = (f32[5,3,8,8]{3,2,1,0:T(8,128)S(1)}, f32[5,3,8,8]{3,2,1,0:T(8,128)S(1)}, u32[]{:S(2)}, u32[]{:S(2)}) collective-permute-start(f32[5,3,8,8]{3,2,1,0:T(8,128)S(1)} %get-tuple-element.264), channel_id=1, source_target_pairs={{0,8},{8,16},{16,24},{1,9},{9,17},{17,25},{2,10},{10,18},{18,26},{... | collective-permute-start | bytes 11528 | tf_op jit(solution)/shard_map/ppermute | solution.py:21
  88.4 25.4 %collective-permute-start.4 = (f32[5,3,8,8]{3,2,1,0:T(8,128)S(1)}, f32[5,3,8,8]{3,2,1,0:T(8,128)S(1)}, u32[]{:S(2)}, u32[]{:S(2)}) collective-permute-start(f32[5,3,8,8]{3,2,1,0:T(8,128)S(1)} %get-tuple-element.265), channel_id=1, source_target_pairs={{8,0},{16,8},{24,16},{9,1},{17,9},{25,17},{10,2},{18,10},{26,18},{... | collective-permute-start | bytes 11528 | tf_op jit(solution)/shard_map/ppermute | solution.py:23
  89.7 30.3 %collective-permute-start.40 = (f32[8,3,8,8]{3,2,1,0:T(8,128)S(1)}, f32[8,3,8,8]{3,2,1,0:T(8,128)S(1)}, u32[]{:S(2)}, u32[]{:S(2)}) collective-permute-start(f32[8,3,8,8]{3,2,1,0:T(8,128)S(1)} %get-tuple-element.192), channel_id=1, source_target_pairs={{8,0},{16,8},{24,16},{9,1},{17,9},{25,17},{10,2},{18,10},{26,18},{... | collective-permute-start | bytes 18440 | tf_op jit(solution)/shard_map/ppermute | solution.py:23
  91.1 8.9 %collective-permute-start.33 = (bf16[5,1,8,8]{3,2,1,0:T(8,128)(2,1)S(1)}, bf16[5,1,8,8]{3,2,1,0:T(8,128)(2,1)S(1)}, u32[]{:S(2)}, u32[]{:S(2)}) collective-permute-start(bf16[5,1,8,8]{3,2,1,0:T(8,128)(2,1)S(1)} %get-tuple-element.303), channel_id=1, source_target_pairs={{8,0},{16,8},{24,16},{9,1},{17,9},{25,17},{10,2},{18,10},{26,18},{... | collective-permute-start | bytes 1928 | tf_op jit(solution)/shard_map/ppermute | solution.py:23
  92.4 7.9 %collective-permute-start.32 = (bf16[5,1,8,8]{3,2,1,0:T(8,128)(2,1)S(1)}, bf16[5,1,8,8]{3,2,1,0:T(8,128)(2,1)S(1)}, u32[]{:S(2)}, u32[]{:S(2)}) collective-permute-start(bf16[5,1,8,8]{3,2,1,0:T(8,128)(2,1)S(1)} %get-tuple-element.302), channel_id=1, source_target_pairs={{0,8},{8,16},{16,24},{1,9},{9,17},{17,25},{2,10},{10,18},{18,26},{... | collective-permute-start | bytes 1928 | tf_op jit(solution)/shard_map/ppermute | solution.py:21
  100.3 6.8 %collective-permute-start.35 = (bf16[5,6,1,8]{3,2,1,0:T(2,128)(2,1)S(1)}, bf16[5,6,1,8]{3,2,1,0:T(2,128)(2,1)S(1)}, u32[]{:S(2)}, u32[]{:S(2)}) collective-permute-start(bf16[5,6,1,8]{3,2,1,0:T(2,128)(2,1)S(1)} %get-tuple-element.285), channel_id=1, source_target_pairs={{1,0},{2,1},{3,2},{4,3},{5,4},{6,5},{7,6},{9,8},{10,9},{11,10},{12... | collective-permute-start | bytes 1448 | tf_op jit(solution)/shard_map/ppermute | solution.py:23
  101.6 9.4 %collective-permute-start.34 = (bf16[5,6,1,8]{3,2,1,0:T(2,128)(2,1)S(1)}, bf16[5,6,1,8]{3,2,1,0:T(2,128)(2,1)S(1)}, u32[]{:S(2)}, u32[]{:S(2)}) collective-permute-start(bf16[5,6,1,8]{3,2,1,0:T(2,128)(2,1)S(1)} %get-tuple-element.284), channel_id=1, source_target_pairs={{0,1},{1,2},{2,3},{3,4},{4,5},{5,6},{6,7},{8,9},{9,10},{10,11},{11... | collective-permute-start | bytes 1448 | tf_op jit(solution)/shard_map/ppermute | solution.py:21
  107.7 12.3 %collective-permute-start.41 = (f32[8,3,8,8]{3,2,1,0:T(8,128)S(1)}, f32[8,3,8,8]{3,2,1,0:T(8,128)S(1)}, u32[]{:S(2)}, u32[]{:S(2)}) collective-permute-start(f32[8,3,8,8]{3,2,1,0:T(8,128)S(1)} %get-tuple-element.191), channel_id=1, source_target_pairs={{0,8},{8,16},{16,24},{1,9},{9,17},{17,25},{2,10},{10,18},{18,26},{... | collective-permute-start | bytes 18440 | tf_op jit(solution)/shard_map/ppermute | solution.py:21
  113.8 12.2 %collective-permute-start.7 = (f32[5,10,3,8]{3,2,1,0:T(4,128)S(1)}, f32[5,10,3,8]{3,2,1,0:T(4,128)S(1)}, u32[]{:S(2)}, u32[]{:S(2)}) collective-permute-start(f32[5,10,3,8]{3,2,1,0:T(4,128)S(1)} %get-tuple-element.149), channel_id=1, source_target_pairs={{0,1},{1,2},{2,3},{3,4},{4,5},{5,6},{6,7},{8,9},{9,10},{10,11},{11... | collective-permute-start | bytes 14408 | tf_op jit(solution)/shard_map/ppermute | solution.py:21
  118.4 7.7 %collective-permute-start.6 = (f32[5,10,3,8]{3,2,1,0:T(4,128)S(1)}, f32[5,10,3,8]{3,2,1,0:T(4,128)S(1)}, u32[]{:S(2)}, u32[]{:S(2)}) collective-permute-start(f32[5,10,3,8]{3,2,1,0:T(4,128)S(1)} %get-tuple-element.148), channel_id=1, source_target_pairs={{1,0},{2,1},{3,2},{4,3},{5,4},{6,5},{7,6},{9,8},{10,9},{11,10},{12... | collective-permute-start | bytes 14408 | tf_op jit(solution)/shard_map/ppermute | solution.py:23
  120.1 20.9 %collective-permute-start.43 = (f32[8,10,3,8]{3,2,1,0:T(4,128)S(1)}, f32[8,10,3,8]{3,2,1,0:T(4,128)S(1)}, u32[]{:S(2)}, u32[]{:S(2)}) collective-permute-start(f32[8,10,3,8]{3,2,1,0:T(4,128)S(1)} %get-tuple-element.91), channel_id=1, source_target_pairs={{0,1},{1,2},{2,3},{3,4},{4,5},{5,6},{6,7},{8,9},{9,10},{10,11},{11... | collective-permute-start | bytes 23048 | tf_op jit(solution)/shard_map/ppermute | solution.py:21
  124.7 16.3 %collective-permute-start.42 = (f32[8,10,3,8]{3,2,1,0:T(4,128)S(1)}, f32[8,10,3,8]{3,2,1,0:T(4,128)S(1)}, u32[]{:S(2)}, u32[]{:S(2)}) collective-permute-start(f32[8,10,3,8]{3,2,1,0:T(4,128)S(1)} %get-tuple-element.90), channel_id=1, source_target_pairs={{1,0},{2,1},{3,2},{4,3},{5,4},{6,5},{7,6},{9,8},{10,9},{11,10},{12... | collective-permute-start | bytes 23048 | tf_op jit(solution)/shard_map/ppermute | solution.py:23
  126.4 5.7 collective-permute-start.9
  133.9 7.7 %collective-permute-start.11 = (f32[5,10,3,8]{3,2,1,0:T(4,128)S(1)}, f32[5,10,3,8]{3,2,1,0:T(4,128)S(1)}, u32[]{:S(2)}, u32[]{:S(2)}) collective-permute-start(f32[5,10,3,8]{3,2,1,0:T(4,128)S(1)} %get-tuple-element.147), channel_id=1, source_target_pairs={{0,1},{1,2},{2,3},{3,4},{4,5},{5,6},{6,7},{8,9},{9,10},{10,11},{11... | collective-permute-start | bytes 14408 | tf_op jit(solution)/shard_map/ppermute | solution.py:21
  139.4 7.5 %collective-permute-start.10 = (f32[5,10,3,8]{3,2,1,0:T(4,128)S(1)}, f32[5,10,3,8]{3,2,1,0:T(4,128)S(1)}, u32[]{:S(2)}, u32[]{:S(2)}) collective-permute-start(f32[5,10,3,8]{3,2,1,0:T(4,128)S(1)} %get-tuple-element.146), channel_id=1, source_target_pairs={{1,0},{2,1},{3,2},{4,3},{5,4},{6,5},{7,6},{9,8},{10,9},{11,10},{12... | collective-permute-start | bytes 14408 | tf_op jit(solution)/shard_map/ppermute | solution.py:23
  147.8 5.4 collective-permute-start.13
  151.4 3.8 collective-permute-start.12
  155.3 11.4 %collective-permute-start.15 = (f32[5,10,3,8]{3,2,1,0:T(4,128)S(1)}, f32[5,10,3,8]{3,2,1,0:T(4,128)S(1)}, u32[]{:S(2)}, u32[]{:S(2)}) collective-permute-start(f32[5,10,3,8]{3,2,1,0:T(4,128)S(1)} %get-tuple-element.145), channel_id=1, source_target_pairs={{0,1},{1,2},{2,3},{3,4},{4,5},{5,6},{6,7},{8,9},{9,10},{10,11},{11... | collective-permute-start | bytes 14408 | tf_op jit(solution)/shard_map/ppermute | solution.py:21
  160.1 6.6 %collective-permute-start.14 = (f32[5,10,3,8]{3,2,1,0:T(4,128)S(1)}, f32[5,10,3,8]{3,2,1,0:T(4,128)S(1)}, u32[]{:S(2)}, u32[]{:S(2)}) collective-permute-start(f32[5,10,3,8]{3,2,1,0:T(4,128)S(1)} %get-tuple-element.144), channel_id=1, source_target_pairs={{1,0},{2,1},{3,2},{4,3},{5,4},{6,5},{7,6},{9,8},{10,9},{11,10},{12... | collective-permute-start | bytes 14408 | tf_op jit(solution)/shard_map/ppermute | solution.py:23
  180.0 24.7 %collective-permute-start.37 = (bf16[64,1,8,8]{0,3,2,1:T(8,128)(2,1)S(1)}, bf16[64,1,8,8]{0,3,2,1:T(8,128)(2,1)S(1)}, u32[]{:S(2)}, u32[]{:S(2)}) collective-permute-start(bf16[64,1,8,8]{0,3,2,1:T(8,128)(2,1)S(1)} %get-tuple-element.281), channel_id=1, source_target_pairs={{8,0},{16,8},{24,16},{9,1},{17,9},{25,17},{10,2},{18,10},{26,18},{... | collective-permute-start | bytes 24584 | tf_op jit(solution)/shard_map/ppermute | solution.py:23
  181.3 23.4 %collective-permute-start.36 = (bf16[64,1,8,8]{0,3,2,1:T(8,128)(2,1)S(1)}, bf16[64,1,8,8]{0,3,2,1:T(8,128)(2,1)S(1)}, u32[]{:S(2)}, u32[]{:S(2)}) collective-permute-start(bf16[64,1,8,8]{0,3,2,1:T(8,128)(2,1)S(1)} %get-tuple-element.280), channel_id=1, source_target_pairs={{0,8},{8,16},{16,24},{1,9},{9,17},{17,25},{2,10},{10,18},{18,26},{... | collective-permute-start | bytes 24584 | tf_op jit(solution)/shard_map/ppermute | solution.py:21
  205.4 7.6 %collective-permute-start.39 = (bf16[64,6,1,8]{0,3,2,1:T(8,128)(2,1)S(1)}, bf16[64,6,1,8]{0,3,2,1:T(8,128)(2,1)S(1)}, u32[]{:S(2)}, u32[]{:S(2)}) collective-permute-start(bf16[64,6,1,8]{0,3,2,1:T(8,128)(2,1)S(1)} %get-tuple-element.228), channel_id=1, source_target_pairs={{1,0},{2,1},{3,2},{4,3},{5,4},{6,5},{7,6},{9,8},{10,9},{11,10},{12... | collective-permute-start | bytes 18440 | tf_op jit(solution)/shard_map/ppermute | solution.py:23
  206.7 6.3 collective-permute-start.38
  214.1 17.3 %collective-permute-start.45 = (bf16[64,1,8,8]{0,3,2,1:T(8,128)(2,1)S(1)}, bf16[64,1,8,8]{0,3,2,1:T(8,128)(2,1)S(1)}, u32[]{:S(2)}, u32[]{:S(2)}) collective-permute-start(bf16[64,1,8,8]{0,3,2,1:T(8,128)(2,1)S(1)} %get-tuple-element.279), channel_id=1, source_target_pairs={{8,0},{16,8},{24,16},{9,1},{17,9},{25,17},{10,2},{18,10},{26,18},{... | collective-permute-start | bytes 24584 | tf_op jit(solution)/shard_map/ppermute | solution.py:23
  215.4 16.0 %collective-permute-start.44 = (bf16[64,1,8,8]{0,3,2,1:T(8,128)(2,1)S(1)}, bf16[64,1,8,8]{0,3,2,1:T(8,128)(2,1)S(1)}, u32[]{:S(2)}, u32[]{:S(2)}) collective-permute-start(bf16[64,1,8,8]{0,3,2,1:T(8,128)(2,1)S(1)} %get-tuple-element.278), channel_id=1, source_target_pairs={{0,8},{8,16},{16,24},{1,9},{9,17},{17,25},{2,10},{10,18},{18,26},{... | collective-permute-start | bytes 24584 | tf_op jit(solution)/shard_map/ppermute | solution.py:21
  231.4 6.5 %collective-permute-start.47 = (bf16[64,6,1,8]{0,3,2,1:T(8,128)(2,1)S(1)}, bf16[64,6,1,8]{0,3,2,1:T(8,128)(2,1)S(1)}, u32[]{:S(2)}, u32[]{:S(2)}) collective-permute-start(bf16[64,6,1,8]{0,3,2,1:T(8,128)(2,1)S(1)} %get-tuple-element.226), channel_id=1, source_target_pairs={{1,0},{2,1},{3,2},{4,3},{5,4},{6,5},{7,6},{9,8},{10,9},{11,10},{12... | collective-permute-start | bytes 18440 | tf_op jit(solution)/shard_map/ppermute | solution.py:23
  232.7 6.1 collective-permute-start.46
  242.9 5.3 collective-permute-start.48
  244.2 4.7 collective-permute-start.49
  249.0 7.7 %collective-permute-start.51 = (f32[8,10,3,8]{3,2,1,0:T(4,128)S(1)}, f32[8,10,3,8]{3,2,1,0:T(4,128)S(1)}, u32[]{:S(2)}, u32[]{:S(2)}) collective-permute-start(f32[8,10,3,8]{3,2,1,0:T(4,128)S(1)} %get-tuple-element.89), channel_id=1, source_target_pairs={{0,1},{1,2},{2,3},{3,4},{4,5},{5,6},{6,7},{8,9},{9,10},{10,11},{11... | collective-permute-start | bytes 23048 | tf_op jit(solution)/shard_map/ppermute | solution.py:21
  253.5 8.4 %collective-permute-start.50 = (f32[8,10,3,8]{3,2,1,0:T(4,128)S(1)}, f32[8,10,3,8]{3,2,1,0:T(4,128)S(1)}, u32[]{:S(2)}, u32[]{:S(2)}) collective-permute-start(f32[8,10,3,8]{3,2,1,0:T(4,128)S(1)} %get-tuple-element.88), channel_id=1, source_target_pairs={{1,0},{2,1},{3,2},{4,3},{5,4},{6,5},{7,6},{9,8},{10,9},{11,10},{12... | collective-permute-start | bytes 23048 | tf_op jit(solution)/shard_map/ppermute | solution.py:23
  263.9 19.7 %collective-permute-start.52 = (f32[8,3,8,8]{3,2,1,0:T(8,128)S(1)}, f32[8,3,8,8]{3,2,1,0:T(8,128)S(1)}, u32[]{:S(2)}, u32[]{:S(2)}) collective-permute-start(f32[8,3,8,8]{3,2,1,0:T(8,128)S(1)} %get-tuple-element.182), channel_id=1, source_target_pairs={{8,0},{16,8},{24,16},{9,1},{17,9},{25,17},{10,2},{18,10},{26,18},{... | collective-permute-start | bytes 18440 | tf_op jit(solution)/shard_map/ppermute | solution.py:23
  265.2 18.4 %collective-permute-start.53 = (f32[8,3,8,8]{3,2,1,0:T(8,128)S(1)}, f32[8,3,8,8]{3,2,1,0:T(8,128)S(1)}, u32[]{:S(2)}, u32[]{:S(2)}) collective-permute-start(f32[8,3,8,8]{3,2,1,0:T(8,128)S(1)} %get-tuple-element.181), channel_id=1, source_target_pairs={{0,8},{8,16},{16,24},{1,9},{9,17},{17,25},{2,10},{10,18},{18,26},{... | collective-permute-start | bytes 18440 | tf_op jit(solution)/shard_map/ppermute | solution.py:21
  269.0 6.9 %collective-permute-start.17 = (f32[5,3,8,8]{3,2,1,0:T(8,128)S(1)}, f32[5,3,8,8]{3,2,1,0:T(8,128)S(1)}, u32[]{:S(2)}, u32[]{:S(2)}) collective-permute-start(f32[5,3,8,8]{3,2,1,0:T(8,128)S(1)} %get-tuple-element.246), channel_id=1, source_target_pairs={{0,8},{8,16},{16,24},{1,9},{9,17},{17,25},{2,10},{10,18},{18,26},{... | collective-permute-start | bytes 11528 | tf_op jit(solution)/shard_map/ppermute | solution.py:21
  277.2 13.1 %collective-permute-start.19 = (f32[5,10,3,8]{3,2,1,0:T(4,128)S(1)}, f32[5,10,3,8]{3,2,1,0:T(4,128)S(1)}, u32[]{:S(2)}, u32[]{:S(2)}) collective-permute-start(f32[5,10,3,8]{3,2,1,0:T(4,128)S(1)} %get-tuple-element.141), channel_id=1, source_target_pairs={{0,1},{1,2},{2,3},{3,4},{4,5},{5,6},{6,7},{8,9},{9,10},{10,11},{11... | collective-permute-start | bytes 14408 | tf_op jit(solution)/shard_map/ppermute | solution.py:21
  282.0 8.3 %collective-permute-start.18 = (f32[5,10,3,8]{3,2,1,0:T(4,128)S(1)}, f32[5,10,3,8]{3,2,1,0:T(4,128)S(1)}, u32[]{:S(2)}, u32[]{:S(2)}) collective-permute-start(f32[5,10,3,8]{3,2,1,0:T(4,128)S(1)} %get-tuple-element.140), channel_id=1, source_target_pairs={{1,0},{2,1},{3,2},{4,3},{5,4},{6,5},{7,6},{9,8},{10,9},{11,10},{12... | collective-permute-start | bytes 14408 | tf_op jit(solution)/shard_map/ppermute | solution.py:23
  283.7 7.8 %collective-permute-start.55 = (f32[8,10,3,8]{3,2,1,0:T(4,128)S(1)}, f32[8,10,3,8]{3,2,1,0:T(4,128)}, u32[]{:S(2)}, u32[]{:S(2)}) collective-permute-start(f32[8,10,3,8]{3,2,1,0:T(4,128)S(1)} %get-tuple-element.87), channel_id=1, source_target_pairs={{0,1},{1,2},{2,3},{3,4},{4,5},{5,6},{6,7},{8,9},{9,10},{10,11},{11... | collective-permute-start | bytes 23048 | tf_op jit(solution)/shard_map/ppermute | solution.py:21
  288.9 8.0 %collective-permute-start.54 = (f32[8,10,3,8]{3,2,1,0:T(4,128)S(1)}, f32[8,10,3,8]{3,2,1,0:T(4,128)}, u32[]{:S(2)}, u32[]{:S(2)}) collective-permute-start(f32[8,10,3,8]{3,2,1,0:T(4,128)S(1)} %get-tuple-element.86), channel_id=1, source_target_pairs={{1,0},{2,1},{3,2},{4,3},{5,4},{6,5},{7,6},{9,8},{10,9},{11,10},{12... | collective-permute-start | bytes 23048 | tf_op jit(solution)/shard_map/ppermute | solution.py:23
  299.9 71.5 %collective-permute-start.21 = (f32[5,3,8,8]{3,2,1,0:T(8,128)}, f32[5,3,8,8]{3,2,1,0:T(8,128)S(1)}, u32[]{:S(2)}, u32[]{:S(2)}) collective-permute-start(f32[5,3,8,8]{3,2,1,0:T(8,128)} %get-tuple-element.243), channel_id=1, source_target_pairs={{0,8},{8,16},{16,24},{1,9},{9,17},{17,25},{2,10},{10,18},{18,26},{... | collective-permute-start | bytes 11528 | tf_op jit(solution)/shard_map/ppermute | solution.py:21
  302.7 68.7 %collective-permute-start.20 = (f32[5,3,8,8]{3,2,1,0:T(8,128)}, f32[5,3,8,8]{3,2,1,0:T(8,128)S(1)}, u32[]{:S(2)}, u32[]{:S(2)}) collective-permute-start(f32[5,3,8,8]{3,2,1,0:T(8,128)} %get-tuple-element.242), channel_id=1, source_target_pairs={{8,0},{16,8},{24,16},{9,1},{17,9},{25,17},{10,2},{18,10},{26,18},{... | collective-permute-start | bytes 11528 | tf_op jit(solution)/shard_map/ppermute | solution.py:23
  304.3 13.8 %collective-permute-start.57 = (bf16[5,1,8,8]{3,2,1,0:T(8,128)(2,1)S(1)}, bf16[5,1,8,8]{3,2,1,0:T(8,128)(2,1)S(1)}, u32[]{:S(2)}, u32[]{:S(2)}) collective-permute-start(bf16[5,1,8,8]{3,2,1,0:T(8,128)(2,1)S(1)} %get-tuple-element.301), channel_id=1, source_target_pairs={{8,0},{16,8},{24,16},{9,1},{17,9},{25,17},{10,2},{18,10},{26,18},{... | collective-permute-start | bytes 1928 | tf_op jit(solution)/shard_map/ppermute | solution.py:23
  305.6 12.5 %collective-permute-start.56 = (bf16[5,1,8,8]{3,2,1,0:T(8,128)(2,1)S(1)}, bf16[5,1,8,8]{3,2,1,0:T(8,128)(2,1)S(1)}, u32[]{:S(2)}, u32[]{:S(2)}) collective-permute-start(bf16[5,1,8,8]{3,2,1,0:T(8,128)(2,1)S(1)} %get-tuple-element.300), channel_id=1, source_target_pairs={{0,8},{8,16},{16,24},{1,9},{9,17},{17,25},{2,10},{10,18},{18,26},{... | collective-permute-start | bytes 1928 | tf_op jit(solution)/shard_map/ppermute | solution.py:21
  318.1 6.8 %collective-permute-start.59 = (bf16[5,6,1,8]{3,2,1,0:T(2,128)(2,1)S(1)}, bf16[5,6,1,8]{3,2,1,0:T(2,128)(2,1)S(1)}, u32[]{:S(2)}, u32[]{:S(2)}) collective-permute-start(bf16[5,6,1,8]{3,2,1,0:T(2,128)(2,1)S(1)} %get-tuple-element.283), channel_id=1, source_target_pairs={{1,0},{2,1},{3,2},{4,3},{5,4},{6,5},{7,6},{9,8},{10,9},{11,10},{12... | collective-permute-start | bytes 1448 | tf_op jit(solution)/shard_map/ppermute | solution.py:23
  319.4 6.0 collective-permute-start.58
  328.2 10.7 %collective-permute-start.61 = (bf16[64,1,8,8]{0,3,2,1:T(8,128)(2,1)S(1)}, bf16[64,1,8,8]{0,3,2,1:T(8,128)(2,1)S(1)}, u32[]{:S(2)}, u32[]{:S(2)}) collective-permute-start(bf16[64,1,8,8]{0,3,2,1:T(8,128)(2,1)S(1)} %get-tuple-element.277), channel_id=1, source_target_pairs={{8,0},{16,8},{24,16},{9,1},{17,9},{25,17},{10,2},{18,10},{26,18},{... | collective-permute-start | bytes 24584 | tf_op jit(solution)/shard_map/ppermute | solution.py:23
  329.5 9.4 %collective-permute-start.60 = (bf16[64,1,8,8]{0,3,2,1:T(8,128)(2,1)S(1)}, bf16[64,1,8,8]{0,3,2,1:T(8,128)(2,1)S(1)}, u32[]{:S(2)}, u32[]{:S(2)}) collective-permute-start(bf16[64,1,8,8]{0,3,2,1:T(8,128)(2,1)S(1)} %get-tuple-element.276), channel_id=1, source_target_pairs={{0,8},{8,16},{16,24},{1,9},{9,17},{17,25},{2,10},{10,18},{18,26},{... | collective-permute-start | bytes 24584 | tf_op jit(solution)/shard_map/ppermute | solution.py:21
  338.9 6.2 collective-permute-start.63
  340.2 6.1 collective-permute-start.62
  369.3 263.5 %all-reduce.4.cloned.1.call-start = ((), (), s32[]{:S(2)}) async-start(), calls=%async_computation | async-start | bytes 1769472 | tf_op jit(solution)/shard_map/psum | solution.py:266
  371.5 8.2 %collective-permute-start.23 = (f32[5,10,3,8]{3,2,1,0:T(4,128)S(1)}, f32[5,10,3,8]{3,2,1,0:T(4,128)S(1)}, u32[]{:S(2)}, u32[]{:S(2)}) collective-permute-start(f32[5,10,3,8]{3,2,1,0:T(4,128)S(1)} %get-tuple-element.139), channel_id=1, source_target_pairs={{0,1},{1,2},{2,3},{3,4},{4,5},{5,6},{6,7},{8,9},{9,10},{10,11},{11... | collective-permute-start | bytes 14408 | tf_op jit(solution)/shard_map/ppermute | solution.py:21
  376.5 8.5 %collective-permute-start.22 = (f32[5,10,3,8]{3,2,1,0:T(4,128)S(1)}, f32[5,10,3,8]{3,2,1,0:T(4,128)S(1)}, u32[]{:S(2)}, u32[]{:S(2)}) collective-permute-start(f32[5,10,3,8]{3,2,1,0:T(4,128)S(1)} %get-tuple-element.138), channel_id=1, source_target_pairs={{1,0},{2,1},{3,2},{4,3},{5,4},{6,5},{7,6},{9,8},{10,9},{11,10},{12... | collective-permute-start | bytes 14408 | tf_op jit(solution)/shard_map/ppermute | solution.py:23
  (108 other events, 347.3 us)
Sparse Core Ops, SparseCore 0:
  369.4 128.6 all-reduce.5
  503.3 129.3 all-reduce.3
where the time goes:
time: 652 us; the launch traced here: 643 us
  waiting for transfers between devices  289 us (44%)
  starting transfers between devices  182 us (28%)
  local copies, waits for them, and re-layouts  68.4 us (10%)
  matrix products  65.6 us (10%)
  other arithmetic  20.1 us (3%)
  between operations  17.5 us (3%)
    psum x2, waiting for transfers between devices, body(): result = lax.psum((totals[0], totals[1], totals[2]), ('gx', 'gy'))  244 us
    ppermute x32, starting transfers between devices, padded_2(): lax.ppermute(tail, axis, [(i, (i + 1) % count) for i in range(ends)])  140 us
    ppermute x32, starting transfers between devices, padded_2(): lax.ppermute(head, axis, [((i + 1) % count, i) for i in range(ends)])  41.7 us
    unnamed x240, local copies, waits for them, and re-layouts  40.9 us
    dot_general x162, matrix products, kernel_grad(): lax.dot_general(flat_grad, window.reshape(channels, -1), (((1,), (1,)), (...  37 us
    ppermute x32, waiting for transfers between devices, padded_2(): lax.ppermute(head, axis, [((i + 1) % count, i) for i in range(ends)])  35.6 us
    conv_general_dilated x11, matrix products, conv_valid(): lax.conv_general_dilated(padded[None], kernel, (1, 1, 1), 'VALID', dimens...  28.6 us
  transfers between devices with their start and end apart: 66, of which 22 were waited for; matrix products, arithmetic and copies ran while one was open for 14% of the time, Pallas kernels for 0%

commit v1 on v0

--- a/solution.py
+++ b/solution.py
@@ -263,7 +263,7 @@
         )
         if step_index > 0:
             adjoint_in = carried + state_grad
-    result = lax.psum((totals[0], totals[1], totals[2]), ("gx", "gy"))
+    result = lax.psum(lax.psum((totals[0], totals[1], totals[2]), "gy"), "gx")
     return (current.reshape(channels, size_x, size_y * NZ), result[0], result[1], result[2])
 
 

time: 652 us -> 614 us (0.942)
  waiting for transfers between devices: 289 us -> 252 us
    psum x2 -> x4, waiting for transfers between devices: 244 us -> 206 us  [body(): result = lax.psum(lax.psum((totals[0], totals[1], totals[2]), 'gy'), 'gx')]
  transfers between devices with their start and end apart: 66 -> 68, of which waited for: 22 -> 24; matrix products, arithmetic and copies ran while one was open for 14% -> 15% of each run, Pallas kernels for 0% -> 0%
where the time goes in v1:
time: 614 us; the launch traced here: 605 us
  waiting for transfers between devices  252 us (41%)
  starting transfers between devices  182 us (30%)
  local copies, waits for them, and re-layouts  68.5 us (11%)
  matrix products  65.6 us (11%)
  other arithmetic  20.1 us (3%)
  between operations  17.2 us (3%)
    psum x4, waiting for transfers between devices, body(): result = lax.psum(lax.psum((totals[0], totals[1], totals[2]), 'gy'), 'gx')  206 us
    ppermute x32, starting transfers between devices, padded_2(): lax.ppermute(tail, axis, [(i, (i + 1) % count) for i in range(ends)])  140 us
    ppermute x32, starting transfers between devices, padded_2(): lax.ppermute(head, axis, [((i + 1) % count, i) for i in range(ends)])  41.7 us
    unnamed x240, local copies, waits for them, and re-layouts  41 us
    dot_general x162, matrix products, kernel_grad(): lax.dot_general(flat_grad, window.reshape(channels, -1), (((1,), (1,)), (...  37 us
    ppermute x32, waiting for transfers between devices, padded_2(): lax.ppermute(head, axis, [((i + 1) % count, i) for i in range(ends)])  35.2 us
    conv_general_dilated x11, matrix products, conv_valid(): lax.conv_general_dilated(padded[None], kernel, (1, 1, 1), 'VALID', dimens...  28.6 us
  transfers between devices with their start and end apart: 68, of which 24 were waited for; matrix products, arithmetic and copies ran while one was open for 15% of the time, Pallas kernels for 0%

profile of v1, /device:TPU:0, one launch (start us, length us, event | category | flops | bytes accessed | tf_op | source)
XLA Modules:
  0.0 604.7 jit_solution(5786832606067728861)
XLA Ops:
  8.0 2.4 collective-permute-start.1
  14.4 5.8 collective-permute-start.25
  24.3 1.9 copy.1395
  30.3 3.4 collective-permute-start.3
  33.7 1.3 collective-permute-start.2
  35.9 5.2 collective-permute-start.27
  44.1 2.1 copy.1387
  46.2 2.5 convolution_tanh_fusion
  49.9 5.2 fusion.164
  58.3 2.8 fusion.175
  64.0 1.7 collective-permute-start.28
  65.7 3.4 collective-permute-start.29
  70.2 4.3 collective-permute-start.31
  75.9 1.7 collective-permute-done.31
  77.6 5.0 collective-permute-done.30
  85.1 3.2 collective-permute-start.5
  88.4 1.3 collective-permute-start.4
  92.4 7.0 %collective-permute-start.32 = (bf16[5,1,8,8]{3,2,1,0:T(8,128)(2,1)S(1)}, bf16[5,1,8,8]{3,2,1,0:T(8,128)(2,1)S(1)}, u32[]{:S(2)}, u32[]{:S(2)}) collective-permute-start(bf16[5,1,8,8]{3,2,1,0:T(8,128)(2,1)S(1)} %get-tuple-element.304), channel_id=1, source_target_pairs={{0,8},{8,16},{16,24},{1,9},{9,17},{17,25},{2,10},{10,18},{18,26},{... | collective-permute-start | bytes 1928 | tf_op jit(solution)/shard_map/ppermute | solution.py:21
  101.6 5.4 collective-permute-start.34
  107.7 3.3 collective-permute-start.41
  112.3 1.4 fusion.898
  113.8 4.5 collective-permute-start.7
  120.1 4.6 collective-permute-start.43
  126.4 3.9 collective-permute-start.9
  132.1 1.8 collective-permute-done.8
  133.9 5.4 collective-permute-start.11
  141.6 5.2 collective-permute-done.10
  147.8 3.7 collective-permute-start.13
  153.2 2.0 collective-permute-done.12
  155.3 4.8 collective-permute-start.15
  162.4 4.3 collective-permute-done.14
  168.9 1.9 copy.1400
  170.8 2.5 fusion.691
  174.6 5.2 fusion.162
  181.3 4.2 collective-permute-start.36
  186.6 2.8 fusion.173
  206.7 4.5 collective-permute-start.38
  215.4 3.7 collective-permute-start.44
  232.7 5.0 collective-permute-start.46
  239.0 2.8 fusion.171
  244.2 3.7 collective-permute-start.49
  249.0 4.5 collective-permute-start.51
  254.9 1.7 collective-permute-done.51
  256.6 5.3 collective-permute-done.50
  265.2 3.6 collective-permute-start.53
  269.0 5.0 collective-permute-start.17
  277.1 4.8 collective-permute-start.19
  283.7 5.2 collective-permute-start.55
  291.5 5.4 collective-permute-done.54
  299.9 2.8 collective-permute-start.21
  305.6 4.4 collective-permute-start.56
  319.4 4.5 collective-permute-start.58
  326.7 1.4 fusion.899
  329.4 3.5 collective-permute-start.60
  340.2 4.7 collective-permute-start.62
  371.6 4.9 collective-permute-start.23
  378.1 1.9 collective-permute-done.23
  380.0 4.9 collective-permute-done.22
  385.5 58.9 %all-reduce.11.cloned.1.call-done = (f32[64,135]{0,1:T(8,128)}, f32[5,1728]{1,0:T(8,128)}) async-done(((f32[64,135]{0,1:T(8,128)}, f32[5,1728]{1,0:T(8,128)}), (f32[64,135]{0,1:T(8,128)}, f32[5,1728]{1,0:T(8,128)})) %all-reduce.11.cloned.1.call-update) | async-done | bytes 69136 | tf_op jit(solution)/shard_map/psum | solution.py:266
  444.5 79.3 %all-reduce.7.cloned.1.call-done = f32[64,1728]{0,1:T(8,128)} async-done(((f32[64,1728]{0,1:T(8,128)}), f32[64,1728]{0,1:T(8,128)}) %all-reduce.7.cloned.1.call-update) | async-done | bytes 442384 | tf_op jit(solution)/shard_map/psum | solution.py:266
  525.3 31.9 %all-reduce.13.cloned.1.call-done = (f32[64,135]{0,1:T(8,128)}, f32[5,1728]{1,0:T(8,128)}) async-done(((f32[64,135]{0,1:T(8,128)}, f32[5,1728]{1,0:T(8,128)}), (f32[64,135]{0,1:T(8,128)}, f32[5,1728]{1,0:T(8,128)})) %all-reduce.13.cloned.1.call-update) | async-done | bytes 69136 | tf_op jit(solution)/shard_map/psum | solution.py:266
  557.1 1.6 copy.1540
  558.7 36.3 %all-reduce.9.cloned.1.call-done = f32[64,1728]{0,1:T(8,128)} async-done(((f32[64,1728]{0,1:T(8,128)}), f32[64,1728]{0,1:T(8,128)}) %all-reduce.9.cloned.1.call-update) | async-done | bytes 442384 | tf_op jit(solution)/shard_map/psum | solution.py:266
  595.0 2.2 copy.1541
  (789 shorter events, 161.2 us)
Async XLA Ops:
  7.2 437.3 %all-reduce.11.cloned.1.call-start = ((), (), s32[]{:S(2)}) async-start(), calls=%async_computation.2 | async-start | bytes 253952 | tf_op jit(solution)/shard_map/psum | solution.py:266
  8.0 21.2 %collective-permute-start.1 = (f32[5,3,8,8]{3,2,1,0:T(8,128)S(1)}, f32[5,3,8,8]{3,2,1,0:T(8,128)S(1)}, u32[]{:S(2)}, u32[]{:S(2)}) collective-permute-start(f32[5,3,8,8]{3,2,1,0:T(8,128)S(1)} %get-tuple-element.275), channel_id=1, source_target_pairs={{0,8},{8,16},{16,24},{1,9},{9,17},{17,25},{2,10},{10,18},{18,26},{... | collective-permute-start | bytes 11528 | tf_op jit(solution)/shard_map/ppermute | solution.py:21
  10.5 19.8 %collective-permute-start = (f32[5,3,8,8]{3,2,1,0:T(8,128)S(1)}, f32[5,3,8,8]{3,2,1,0:T(8,128)S(1)}, u32[]{:S(2)}, u32[]{:S(2)}) collective-permute-start(f32[5,3,8,8]{3,2,1,0:T(8,128)S(1)} %get-tuple-element.274), channel_id=1, source_target_pairs={{8,0},{16,8},{24,16},{9,1},{17,9},{25,17},{10,2},{18,10},{26,18},{... | collective-permute-start | bytes 11528 | tf_op jit(solution)/shard_map/ppermute | solution.py:23
  13.1 21.9 %collective-permute-start.24 = (f32[8,3,8,8]{3,2,1,0:T(8,128)S(1)}, f32[8,3,8,8]{3,2,1,0:T(8,128)S(1)}, u32[]{:S(2)}, u32[]{:S(2)}) collective-permute-start(f32[8,3,8,8]{3,2,1,0:T(8,128)S(1)} %get-tuple-element.204), channel_id=1, source_target_pairs={{8,0},{16,8},{24,16},{9,1},{17,9},{25,17},{10,2},{18,10},{26,18},{... | collective-permute-start | bytes 18440 | tf_op jit(solution)/shard_map/ppermute | solution.py:23
  14.4 20.6 %collective-permute-start.25 = (f32[8,3,8,8]{3,2,1,0:T(8,128)S(1)}, f32[8,3,8,8]{3,2,1,0:T(8,128)S(1)}, u32[]{:S(2)}, u32[]{:S(2)}) collective-permute-start(f32[8,3,8,8]{3,2,1,0:T(8,128)S(1)} %get-tuple-element.203), channel_id=1, source_target_pairs={{0,8},{8,16},{16,24},{1,9},{9,17},{17,25},{2,10},{10,18},{18,26},{... | collective-permute-start | bytes 18440 | tf_op jit(solution)/shard_map/ppermute | solution.py:21
  30.3 12.2 %collective-permute-start.3 = (f32[5,10,3,8]{3,2,1,0:T(4,128)S(1)}, f32[5,10,3,8]{3,2,1,0:T(4,128)S(1)}, u32[]{:S(2)}, u32[]{:S(2)}) collective-permute-start(f32[5,10,3,8]{3,2,1,0:T(4,128)S(1)} %get-tuple-element.155), channel_id=1, source_target_pairs={{0,1},{1,2},{2,3},{3,4},{4,5},{5,6},{6,7},{8,9},{9,10},{10,11},{11... | collective-permute-start | bytes 14408 | tf_op jit(solution)/shard_map/ppermute | solution.py:21
  33.7 8.7 %collective-permute-start.2 = (f32[5,10,3,8]{3,2,1,0:T(4,128)S(1)}, f32[5,10,3,8]{3,2,1,0:T(4,128)S(1)}, u32[]{:S(2)}, u32[]{:S(2)}) collective-permute-start(f32[5,10,3,8]{3,2,1,0:T(4,128)S(1)} %get-tuple-element.154), channel_id=1, source_target_pairs={{1,0},{2,1},{3,2},{4,3},{5,4},{6,5},{7,6},{9,8},{10,9},{11,10},{12... | collective-permute-start | bytes 14408 | tf_op jit(solution)/shard_map/ppermute | solution.py:23
  35.9 27.0 %collective-permute-start.27 = (f32[8,10,3,8]{3,2,1,0:T(4,128)}, f32[8,10,3,8]{3,2,1,0:T(4,128)}, u32[]{:S(2)}, u32[]{:S(2)}) collective-permute-start(f32[8,10,3,8]{3,2,1,0:T(4,128)} %get-tuple-element.97), channel_id=1, source_target_pairs={{0,1},{1,2},{2,3},{3,4},{4,5},{5,6},{6,7},{8,9},{9,10},{10,11},{11... | collective-permute-start | bytes 23048 | tf_op jit(solution)/shard_map/ppermute | solution.py:21
  41.1 21.8 %collective-permute-start.26 = (f32[8,10,3,8]{3,2,1,0:T(4,128)}, f32[8,10,3,8]{3,2,1,0:T(4,128)}, u32[]{:S(2)}, u32[]{:S(2)}) collective-permute-start(f32[8,10,3,8]{3,2,1,0:T(4,128)} %get-tuple-element.96), channel_id=1, source_target_pairs={{1,0},{2,1},{3,2},{4,3},{5,4},{6,5},{7,6},{9,8},{10,9},{11,10},{12... | collective-permute-start | bytes 23048 | tf_op jit(solution)/shard_map/ppermute | solution.py:23
  64.0 5.4 collective-permute-start.28
  70.2 7.4 %collective-permute-start.31 = (f32[8,10,3,8]{3,2,1,0:T(4,128)S(1)}, f32[8,10,3,8]{3,2,1,0:T(4,128)S(1)}, u32[]{:S(2)}, u32[]{:S(2)}) collective-permute-start(f32[8,10,3,8]{3,2,1,0:T(4,128)S(1)} %get-tuple-element.95), channel_id=1, source_target_pairs={{0,1},{1,2},{2,3},{3,4},{4,5},{5,6},{6,7},{8,9},{9,10},{10,11},{11... | collective-permute-start | bytes 23048 | tf_op jit(solution)/shard_map/ppermute | solution.py:21
  74.5 8.1 %collective-permute-start.30 = (f32[8,10,3,8]{3,2,1,0:T(4,128)S(1)}, f32[8,10,3,8]{3,2,1,0:T(4,128)S(1)}, u32[]{:S(2)}, u32[]{:S(2)}) collective-permute-start(f32[8,10,3,8]{3,2,1,0:T(4,128)S(1)} %get-tuple-element.94), channel_id=1, source_target_pairs={{1,0},{2,1},{3,2},{4,3},{5,4},{6,5},{7,6},{9,8},{10,9},{11,10},{12... | collective-permute-start | bytes 23048 | tf_op jit(solution)/shard_map/ppermute | solution.py:23
  85.1 28.6 %collective-permute-start.5 = (f32[5,3,8,8]{3,2,1,0:T(8,128)S(1)}, f32[5,3,8,8]{3,2,1,0:T(8,128)S(1)}, u32[]{:S(2)}, u32[]{:S(2)}) collective-permute-start(f32[5,3,8,8]{3,2,1,0:T(8,128)S(1)} %get-tuple-element.266), channel_id=1, source_target_pairs={{0,8},{8,16},{16,24},{1,9},{9,17},{17,25},{2,10},{10,18},{18,26},{... | collective-permute-start | bytes 11528 | tf_op jit(solution)/shard_map/ppermute | solution.py:21
  88.4 25.4 %collective-permute-start.4 = (f32[5,3,8,8]{3,2,1,0:T(8,128)S(1)}, f32[5,3,8,8]{3,2,1,0:T(8,128)S(1)}, u32[]{:S(2)}, u32[]{:S(2)}) collective-permute-start(f32[5,3,8,8]{3,2,1,0:T(8,128)S(1)} %get-tuple-element.267), channel_id=1, source_target_pairs={{8,0},{16,8},{24,16},{9,1},{17,9},{25,17},{10,2},{18,10},{26,18},{... | collective-permute-start | bytes 11528 | tf_op jit(solution)/shard_map/ppermute | solution.py:23
  89.7 30.3 %collective-permute-start.40 = (f32[8,3,8,8]{3,2,1,0:T(8,128)S(1)}, f32[8,3,8,8]{3,2,1,0:T(8,128)S(1)}, u32[]{:S(2)}, u32[]{:S(2)}) collective-permute-start(f32[8,3,8,8]{3,2,1,0:T(8,128)S(1)} %get-tuple-element.194), channel_id=1, source_target_pairs={{8,0},{16,8},{24,16},{9,1},{17,9},{25,17},{10,2},{18,10},{26,18},{... | collective-permute-start | bytes 18440 | tf_op jit(solution)/shard_map/ppermute | solution.py:23
  91.1 8.9 %collective-permute-start.33 = (bf16[5,1,8,8]{3,2,1,0:T(8,128)(2,1)S(1)}, bf16[5,1,8,8]{3,2,1,0:T(8,128)(2,1)S(1)}, u32[]{:S(2)}, u32[]{:S(2)}) collective-permute-start(bf16[5,1,8,8]{3,2,1,0:T(8,128)(2,1)S(1)} %get-tuple-element.305), channel_id=1, source_target_pairs={{8,0},{16,8},{24,16},{9,1},{17,9},{25,17},{10,2},{18,10},{26,18},{... | collective-permute-start | bytes 1928 | tf_op jit(solution)/shard_map/ppermute | solution.py:23
  92.4 7.9 %collective-permute-start.32 = (bf16[5,1,8,8]{3,2,1,0:T(8,128)(2,1)S(1)}, bf16[5,1,8,8]{3,2,1,0:T(8,128)(2,1)S(1)}, u32[]{:S(2)}, u32[]{:S(2)}) collective-permute-start(bf16[5,1,8,8]{3,2,1,0:T(8,128)(2,1)S(1)} %get-tuple-element.304), channel_id=1, source_target_pairs={{0,8},{8,16},{16,24},{1,9},{9,17},{17,25},{2,10},{10,18},{18,26},{... | collective-permute-start | bytes 1928 | tf_op jit(solution)/shard_map/ppermute | solution.py:21
  100.3 6.8 %collective-permute-start.35 = (bf16[5,6,1,8]{3,2,1,0:T(2,128)(2,1)S(1)}, bf16[5,6,1,8]{3,2,1,0:T(2,128)(2,1)S(1)}, u32[]{:S(2)}, u32[]{:S(2)}) collective-permute-start(bf16[5,6,1,8]{3,2,1,0:T(2,128)(2,1)S(1)} %get-tuple-element.287), channel_id=1, source_target_pairs={{1,0},{2,1},{3,2},{4,3},{5,4},{6,5},{7,6},{9,8},{10,9},{11,10},{12... | collective-permute-start | bytes 1448 | tf_op jit(solution)/shard_map/ppermute | solution.py:23
  101.6 9.4 %collective-permute-start.34 = (bf16[5,6,1,8]{3,2,1,0:T(2,128)(2,1)S(1)}, bf16[5,6,1,8]{3,2,1,0:T(2,128)(2,1)S(1)}, u32[]{:S(2)}, u32[]{:S(2)}) collective-permute-start(bf16[5,6,1,8]{3,2,1,0:T(2,128)(2,1)S(1)} %get-tuple-element.286), channel_id=1, source_target_pairs={{0,1},{1,2},{2,3},{3,4},{4,5},{5,6},{6,7},{8,9},{9,10},{10,11},{11... | collective-permute-start | bytes 1448 | tf_op jit(solution)/shard_map/ppermute | solution.py:21
  107.7 12.3 %collective-permute-start.41 = (f32[8,3,8,8]{3,2,1,0:T(8,128)S(1)}, f32[8,3,8,8]{3,2,1,0:T(8,128)S(1)}, u32[]{:S(2)}, u32[]{:S(2)}) collective-permute-start(f32[8,3,8,8]{3,2,1,0:T(8,128)S(1)} %get-tuple-element.193), channel_id=1, source_target_pairs={{0,8},{8,16},{16,24},{1,9},{9,17},{17,25},{2,10},{10,18},{18,26},{... | collective-permute-start | bytes 18440 | tf_op jit(solution)/shard_map/ppermute | solution.py:21
  113.8 12.2 %collective-permute-start.7 = (f32[5,10,3,8]{3,2,1,0:T(4,128)S(1)}, f32[5,10,3,8]{3,2,1,0:T(4,128)S(1)}, u32[]{:S(2)}, u32[]{:S(2)}) collective-permute-start(f32[5,10,3,8]{3,2,1,0:T(4,128)S(1)} %get-tuple-element.151), channel_id=1, source_target_pairs={{0,1},{1,2},{2,3},{3,4},{4,5},{5,6},{6,7},{8,9},{9,10},{10,11},{11... | collective-permute-start | bytes 14408 | tf_op jit(solution)/shard_map/ppermute | solution.py:21
  118.4 7.7 %collective-permute-start.6 = (f32[5,10,3,8]{3,2,1,0:T(4,128)S(1)}, f32[5,10,3,8]{3,2,1,0:T(4,128)S(1)}, u32[]{:S(2)}, u32[]{:S(2)}) collective-permute-start(f32[5,10,3,8]{3,2,1,0:T(4,128)S(1)} %get-tuple-element.150), channel_id=1, source_target_pairs={{1,0},{2,1},{3,2},{4,3},{5,4},{6,5},{7,6},{9,8},{10,9},{11,10},{12... | collective-permute-start | bytes 14408 | tf_op jit(solution)/shard_map/ppermute | solution.py:23
  120.1 20.9 %collective-permute-start.43 = (f32[8,10,3,8]{3,2,1,0:T(4,128)S(1)}, f32[8,10,3,8]{3,2,1,0:T(4,128)S(1)}, u32[]{:S(2)}, u32[]{:S(2)}) collective-permute-start(f32[8,10,3,8]{3,2,1,0:T(4,128)S(1)} %get-tuple-element.93), channel_id=1, source_target_pairs={{0,1},{1,2},{2,3},{3,4},{4,5},{5,6},{6,7},{8,9},{9,10},{10,11},{11... | collective-permute-start | bytes 23048 | tf_op jit(solution)/shard_map/ppermute | solution.py:21
  124.7 16.3 %collective-permute-start.42 = (f32[8,10,3,8]{3,2,1,0:T(4,128)S(1)}, f32[8,10,3,8]{3,2,1,0:T(4,128)S(1)}, u32[]{:S(2)}, u32[]{:S(2)}) collective-permute-start(f32[8,10,3,8]{3,2,1,0:T(4,128)S(1)} %get-tuple-element.92), channel_id=1, source_target_pairs={{1,0},{2,1},{3,2},{4,3},{5,4},{6,5},{7,6},{9,8},{10,9},{11,10},{12... | collective-permute-start | bytes 23048 | tf_op jit(solution)/shard_map/ppermute | solution.py:23
  126.4 5.7 collective-permute-start.9
  133.9 7.7 %collective-permute-start.11 = (f32[5,10,3,8]{3,2,1,0:T(4,128)S(1)}, f32[5,10,3,8]{3,2,1,0:T(4,128)S(1)}, u32[]{:S(2)}, u32[]{:S(2)}) collective-permute-start(f32[5,10,3,8]{3,2,1,0:T(4,128)S(1)} %get-tuple-element.149), channel_id=1, source_target_pairs={{0,1},{1,2},{2,3},{3,4},{4,5},{5,6},{6,7},{8,9},{9,10},{10,11},{11... | collective-permute-start | bytes 14408 | tf_op jit(solution)/shard_map/ppermute | solution.py:21
  139.4 7.5 %collective-permute-start.10 = (f32[5,10,3,8]{3,2,1,0:T(4,128)S(1)}, f32[5,10,3,8]{3,2,1,0:T(4,128)S(1)}, u32[]{:S(2)}, u32[]{:S(2)}) collective-permute-start(f32[5,10,3,8]{3,2,1,0:T(4,128)S(1)} %get-tuple-element.148), channel_id=1, source_target_pairs={{1,0},{2,1},{3,2},{4,3},{5,4},{6,5},{7,6},{9,8},{10,9},{11,10},{12... | collective-permute-start | bytes 14408 | tf_op jit(solution)/shard_map/ppermute | solution.py:23
  147.8 5.4 collective-permute-start.13
  155.3 11.4 %collective-permute-start.15 = (f32[5,10,3,8]{3,2,1,0:T(4,128)S(1)}, f32[5,10,3,8]{3,2,1,0:T(4,128)S(1)}, u32[]{:S(2)}, u32[]{:S(2)}) collective-permute-start(f32[5,10,3,8]{3,2,1,0:T(4,128)S(1)} %get-tuple-element.147), channel_id=1, source_target_pairs={{0,1},{1,2},{2,3},{3,4},{4,5},{5,6},{6,7},{8,9},{9,10},{10,11},{11... | collective-permute-start | bytes 14408 | tf_op jit(solution)/shard_map/ppermute | solution.py:21
  160.1 6.6 %collective-permute-start.14 = (f32[5,10,3,8]{3,2,1,0:T(4,128)S(1)}, f32[5,10,3,8]{3,2,1,0:T(4,128)S(1)}, u32[]{:S(2)}, u32[]{:S(2)}) collective-permute-start(f32[5,10,3,8]{3,2,1,0:T(4,128)S(1)} %get-tuple-element.146), channel_id=1, source_target_pairs={{1,0},{2,1},{3,2},{4,3},{5,4},{6,5},{7,6},{9,8},{10,9},{11,10},{12... | collective-permute-start | bytes 14408 | tf_op jit(solution)/shard_map/ppermute | solution.py:23
  180.0 24.7 %collective-permute-start.37 = (bf16[64,1,8,8]{0,3,2,1:T(8,128)(2,1)S(1)}, bf16[64,1,8,8]{0,3,2,1:T(8,128)(2,1)S(1)}, u32[]{:S(2)}, u32[]{:S(2)}) collective-permute-start(bf16[64,1,8,8]{0,3,2,1:T(8,128)(2,1)S(1)} %get-tuple-element.283), channel_id=1, source_target_pairs={{8,0},{16,8},{24,16},{9,1},{17,9},{25,17},{10,2},{18,10},{26,18},{... | collective-permute-start | bytes 24584 | tf_op jit(solution)/shard_map/ppermute | solution.py:23
  181.3 23.4 %collective-permute-start.36 = (bf16[64,1,8,8]{0,3,2,1:T(8,128)(2,1)S(1)}, bf16[64,1,8,8]{0,3,2,1:T(8,128)(2,1)S(1)}, u32[]{:S(2)}, u32[]{:S(2)}) collective-permute-start(bf16[64,1,8,8]{0,3,2,1:T(8,128)(2,1)S(1)} %get-tuple-element.282), channel_id=1, source_target_pairs={{0,8},{8,16},{16,24},{1,9},{9,17},{17,25},{2,10},{10,18},{18,26},{... | collective-permute-start | bytes 24584 | tf_op jit(solution)/shard_map/ppermute | solution.py:21
  205.4 7.6 %collective-permute-start.39 = (bf16[64,6,1,8]{0,3,2,1:T(8,128)(2,1)S(1)}, bf16[64,6,1,8]{0,3,2,1:T(8,128)(2,1)S(1)}, u32[]{:S(2)}, u32[]{:S(2)}) collective-permute-start(bf16[64,6,1,8]{0,3,2,1:T(8,128)(2,1)S(1)} %get-tuple-element.230), channel_id=1, source_target_pairs={{1,0},{2,1},{3,2},{4,3},{5,4},{6,5},{7,6},{9,8},{10,9},{11,10},{12... | collective-permute-start | bytes 18440 | tf_op jit(solution)/shard_map/ppermute | solution.py:23
  206.7 6.3 %collective-permute-start.38 = (bf16[64,6,1,8]{0,3,2,1:T(8,128)(2,1)S(1)}, bf16[64,6,1,8]{0,3,2,1:T(8,128)(2,1)S(1)}, u32[]{:S(2)}, u32[]{:S(2)}) collective-permute-start(bf16[64,6,1,8]{0,3,2,1:T(8,128)(2,1)S(1)} %get-tuple-element.229), channel_id=1, source_target_pairs={{0,1},{1,2},{2,3},{3,4},{4,5},{5,6},{6,7},{8,9},{9,10},{10,11},{11... | collective-permute-start | bytes 18440 | tf_op jit(solution)/shard_map/ppermute | solution.py:21
  214.1 17.3 %collective-permute-start.45 = (bf16[64,1,8,8]{0,3,2,1:T(8,128)(2,1)S(1)}, bf16[64,1,8,8]{0,3,2,1:T(8,128)(2,1)S(1)}, u32[]{:S(2)}, u32[]{:S(2)}) collective-permute-start(bf16[64,1,8,8]{0,3,2,1:T(8,128)(2,1)S(1)} %get-tuple-element.281), channel_id=1, source_target_pairs={{8,0},{16,8},{24,16},{9,1},{17,9},{25,17},{10,2},{18,10},{26,18},{... | collective-permute-start | bytes 24584 | tf_op jit(solution)/shard_map/ppermute | solution.py:23
  215.4 16.0 %collective-permute-start.44 = (bf16[64,1,8,8]{0,3,2,1:T(8,128)(2,1)S(1)}, bf16[64,1,8,8]{0,3,2,1:T(8,128)(2,1)S(1)}, u32[]{:S(2)}, u32[]{:S(2)}) collective-permute-start(bf16[64,1,8,8]{0,3,2,1:T(8,128)(2,1)S(1)} %get-tuple-element.280), channel_id=1, source_target_pairs={{0,8},{8,16},{16,24},{1,9},{9,17},{17,25},{2,10},{10,18},{18,26},{... | collective-permute-start | bytes 24584 | tf_op jit(solution)/shard_map/ppermute | solution.py:21
  231.4 6.5 %collective-permute-start.47 = (bf16[64,6,1,8]{0,3,2,1:T(8,128)(2,1)S(1)}, bf16[64,6,1,8]{0,3,2,1:T(8,128)(2,1)S(1)}, u32[]{:S(2)}, u32[]{:S(2)}) collective-permute-start(bf16[64,6,1,8]{0,3,2,1:T(8,128)(2,1)S(1)} %get-tuple-element.228), channel_id=1, source_target_pairs={{1,0},{2,1},{3,2},{4,3},{5,4},{6,5},{7,6},{9,8},{10,9},{11,10},{12... | collective-permute-start | bytes 18440 | tf_op jit(solution)/shard_map/ppermute | solution.py:23
  232.7 6.1 %collective-permute-start.46 = (bf16[64,6,1,8]{0,3,2,1:T(8,128)(2,1)S(1)}, bf16[64,6,1,8]{0,3,2,1:T(8,128)(2,1)S(1)}, u32[]{:S(2)}, u32[]{:S(2)}) collective-permute-start(bf16[64,6,1,8]{0,3,2,1:T(8,128)(2,1)S(1)} %get-tuple-element.227), channel_id=1, source_target_pairs={{0,1},{1,2},{2,3},{3,4},{4,5},{5,6},{6,7},{8,9},{9,10},{10,11},{11... | collective-permute-start | bytes 18440 | tf_op jit(solution)/shard_map/ppermute | solution.py:21
  242.9 5.3 collective-permute-start.48
  244.2 4.7 collective-permute-start.49
  249.0 7.7 %collective-permute-start.51 = (f32[8,10,3,8]{3,2,1,0:T(4,128)S(1)}, f32[8,10,3,8]{3,2,1,0:T(4,128)S(1)}, u32[]{:S(2)}, u32[]{:S(2)}) collective-permute-start(f32[8,10,3,8]{3,2,1,0:T(4,128)S(1)} %get-tuple-element.91), channel_id=1, source_target_pairs={{0,1},{1,2},{2,3},{3,4},{4,5},{5,6},{6,7},{8,9},{9,10},{10,11},{11... | collective-permute-start | bytes 23048 | tf_op jit(solution)/shard_map/ppermute | solution.py:21
  253.5 8.4 %collective-permute-start.50 = (f32[8,10,3,8]{3,2,1,0:T(4,128)S(1)}, f32[8,10,3,8]{3,2,1,0:T(4,128)S(1)}, u32[]{:S(2)}, u32[]{:S(2)}) collective-permute-start(f32[8,10,3,8]{3,2,1,0:T(4,128)S(1)} %get-tuple-element.90), channel_id=1, source_target_pairs={{1,0},{2,1},{3,2},{4,3},{5,4},{6,5},{7,6},{9,8},{10,9},{11,10},{12... | collective-permute-start | bytes 23048 | tf_op jit(solution)/shard_map/ppermute | solution.py:23
  263.9 19.7 %collective-permute-start.52 = (f32[8,3,8,8]{3,2,1,0:T(8,128)S(1)}, f32[8,3,8,8]{3,2,1,0:T(8,128)S(1)}, u32[]{:S(2)}, u32[]{:S(2)}) collective-permute-start(f32[8,3,8,8]{3,2,1,0:T(8,128)S(1)} %get-tuple-element.184), channel_id=1, source_target_pairs={{8,0},{16,8},{24,16},{9,1},{17,9},{25,17},{10,2},{18,10},{26,18},{... | collective-permute-start | bytes 18440 | tf_op jit(solution)/shard_map/ppermute | solution.py:23
  265.2 18.4 %collective-permute-start.53 = (f32[8,3,8,8]{3,2,1,0:T(8,128)S(1)}, f32[8,3,8,8]{3,2,1,0:T(8,128)S(1)}, u32[]{:S(2)}, u32[]{:S(2)}) collective-permute-start(f32[8,3,8,8]{3,2,1,0:T(8,128)S(1)} %get-tuple-element.183), channel_id=1, source_target_pairs={{0,8},{8,16},{16,24},{1,9},{9,17},{17,25},{2,10},{10,18},{18,26},{... | collective-permute-start | bytes 18440 | tf_op jit(solution)/shard_map/ppermute | solution.py:21
  269.0 6.9 %collective-permute-start.17 = (f32[5,3,8,8]{3,2,1,0:T(8,128)S(1)}, f32[5,3,8,8]{3,2,1,0:T(8,128)S(1)}, u32[]{:S(2)}, u32[]{:S(2)}) collective-permute-start(f32[5,3,8,8]{3,2,1,0:T(8,128)S(1)} %get-tuple-element.248), channel_id=1, source_target_pairs={{0,8},{8,16},{16,24},{1,9},{9,17},{17,25},{2,10},{10,18},{18,26},{... | collective-permute-start | bytes 11528 | tf_op jit(solution)/shard_map/ppermute | solution.py:21
  277.1 13.1 %collective-permute-start.19 = (f32[5,10,3,8]{3,2,1,0:T(4,128)S(1)}, f32[5,10,3,8]{3,2,1,0:T(4,128)S(1)}, u32[]{:S(2)}, u32[]{:S(2)}) collective-permute-start(f32[5,10,3,8]{3,2,1,0:T(4,128)S(1)} %get-tuple-element.143), channel_id=1, source_target_pairs={{0,1},{1,2},{2,3},{3,4},{4,5},{5,6},{6,7},{8,9},{9,10},{10,11},{11... | collective-permute-start | bytes 14408 | tf_op jit(solution)/shard_map/ppermute | solution.py:21
  282.0 8.3 %collective-permute-start.18 = (f32[5,10,3,8]{3,2,1,0:T(4,128)S(1)}, f32[5,10,3,8]{3,2,1,0:T(4,128)S(1)}, u32[]{:S(2)}, u32[]{:S(2)}) collective-permute-start(f32[5,10,3,8]{3,2,1,0:T(4,128)S(1)} %get-tuple-element.142), channel_id=1, source_target_pairs={{1,0},{2,1},{3,2},{4,3},{5,4},{6,5},{7,6},{9,8},{10,9},{11,10},{12... | collective-permute-start | bytes 14408 | tf_op jit(solution)/shard_map/ppermute | solution.py:23
  283.7 7.8 %collective-permute-start.55 = (f32[8,10,3,8]{3,2,1,0:T(4,128)S(1)}, f32[8,10,3,8]{3,2,1,0:T(4,128)}, u32[]{:S(2)}, u32[]{:S(2)}) collective-permute-start(f32[8,10,3,8]{3,2,1,0:T(4,128)S(1)} %get-tuple-element.89), channel_id=1, source_target_pairs={{0,1},{1,2},{2,3},{3,4},{4,5},{5,6},{6,7},{8,9},{9,10},{10,11},{11... | collective-permute-start | bytes 23048 | tf_op jit(solution)/shard_map/ppermute | solution.py:21
  288.9 8.0 %collective-permute-start.54 = (f32[8,10,3,8]{3,2,1,0:T(4,128)S(1)}, f32[8,10,3,8]{3,2,1,0:T(4,128)}, u32[]{:S(2)}, u32[]{:S(2)}) collective-permute-start(f32[8,10,3,8]{3,2,1,0:T(4,128)S(1)} %get-tuple-element.88), channel_id=1, source_target_pairs={{1,0},{2,1},{3,2},{4,3},{5,4},{6,5},{7,6},{9,8},{10,9},{11,10},{12... | collective-permute-start | bytes 23048 | tf_op jit(solution)/shard_map/ppermute | solution.py:23
  299.9 71.6 %collective-permute-start.21 = (f32[5,3,8,8]{3,2,1,0:T(8,128)}, f32[5,3,8,8]{3,2,1,0:T(8,128)S(1)}, u32[]{:S(2)}, u32[]{:S(2)}) collective-permute-start(f32[5,3,8,8]{3,2,1,0:T(8,128)} %get-tuple-element.245), channel_id=1, source_target_pairs={{0,8},{8,16},{16,24},{1,9},{9,17},{17,25},{2,10},{10,18},{18,26},{... | collective-permute-start | bytes 11528 | tf_op jit(solution)/shard_map/ppermute | solution.py:21
  302.7 68.8 %collective-permute-start.20 = (f32[5,3,8,8]{3,2,1,0:T(8,128)}, f32[5,3,8,8]{3,2,1,0:T(8,128)S(1)}, u32[]{:S(2)}, u32[]{:S(2)}) collective-permute-start(f32[5,3,8,8]{3,2,1,0:T(8,128)} %get-tuple-element.244), channel_id=1, source_target_pairs={{8,0},{16,8},{24,16},{9,1},{17,9},{25,17},{10,2},{18,10},{26,18},{... | collective-permute-start | bytes 11528 | tf_op jit(solution)/shard_map/ppermute | solution.py:23
  304.3 13.8 %collective-permute-start.57 = (bf16[5,1,8,8]{3,2,1,0:T(8,128)(2,1)S(1)}, bf16[5,1,8,8]{3,2,1,0:T(8,128)(2,1)S(1)}, u32[]{:S(2)}, u32[]{:S(2)}) collective-permute-start(bf16[5,1,8,8]{3,2,1,0:T(8,128)(2,1)S(1)} %get-tuple-element.303), channel_id=1, source_target_pairs={{8,0},{16,8},{24,16},{9,1},{17,9},{25,17},{10,2},{18,10},{26,18},{... | collective-permute-start | bytes 1928 | tf_op jit(solution)/shard_map/ppermute | solution.py:23
  305.6 12.5 %collective-permute-start.56 = (bf16[5,1,8,8]{3,2,1,0:T(8,128)(2,1)S(1)}, bf16[5,1,8,8]{3,2,1,0:T(8,128)(2,1)S(1)}, u32[]{:S(2)}, u32[]{:S(2)}) collective-permute-start(bf16[5,1,8,8]{3,2,1,0:T(8,128)(2,1)S(1)} %get-tuple-element.302), channel_id=1, source_target_pairs={{0,8},{8,16},{16,24},{1,9},{9,17},{17,25},{2,10},{10,18},{18,26},{... | collective-permute-start | bytes 1928 | tf_op jit(solution)/shard_map/ppermute | solution.py:21
  318.1 6.8 %collective-permute-start.59 = (bf16[5,6,1,8]{3,2,1,0:T(2,128)(2,1)S(1)}, bf16[5,6,1,8]{3,2,1,0:T(2,128)(2,1)S(1)}, u32[]{:S(2)}, u32[]{:S(2)}) collective-permute-start(bf16[5,6,1,8]{3,2,1,0:T(2,128)(2,1)S(1)} %get-tuple-element.285), channel_id=1, source_target_pairs={{1,0},{2,1},{3,2},{4,3},{5,4},{6,5},{7,6},{9,8},{10,9},{11,10},{12... | collective-permute-start | bytes 1448 | tf_op jit(solution)/shard_map/ppermute | solution.py:23
  319.4 6.0 collective-permute-start.58
  328.1 10.7 %collective-permute-start.61 = (bf16[64,1,8,8]{0,3,2,1:T(8,128)(2,1)S(1)}, bf16[64,1,8,8]{0,3,2,1:T(8,128)(2,1)S(1)}, u32[]{:S(2)}, u32[]{:S(2)}) collective-permute-start(bf16[64,1,8,8]{0,3,2,1:T(8,128)(2,1)S(1)} %get-tuple-element.279), channel_id=1, source_target_pairs={{8,0},{16,8},{24,16},{9,1},{17,9},{25,17},{10,2},{18,10},{26,18},{... | collective-permute-start | bytes 24584 | tf_op jit(solution)/shard_map/ppermute | solution.py:23
  329.4 9.4 %collective-permute-start.60 = (bf16[64,1,8,8]{0,3,2,1:T(8,128)(2,1)S(1)}, bf16[64,1,8,8]{0,3,2,1:T(8,128)(2,1)S(1)}, u32[]{:S(2)}, u32[]{:S(2)}) collective-permute-start(bf16[64,1,8,8]{0,3,2,1:T(8,128)(2,1)S(1)} %get-tuple-element.278), channel_id=1, source_target_pairs={{0,8},{8,16},{16,24},{1,9},{9,17},{17,25},{2,10},{10,18},{18,26},{... | collective-permute-start | bytes 24584 | tf_op jit(solution)/shard_map/ppermute | solution.py:21
  338.9 6.2 %collective-permute-start.63 = (bf16[64,6,1,8]{0,3,2,1:T(8,128)(2,1)S(1)}, bf16[64,6,1,8]{0,3,2,1:T(8,128)(2,1)S(1)}, u32[]{:S(2)}, u32[]{:S(2)}) collective-permute-start(bf16[64,6,1,8]{0,3,2,1:T(8,128)(2,1)S(1)} %get-tuple-element.226), channel_id=1, source_target_pairs={{1,0},{2,1},{3,2},{4,3},{5,4},{6,5},{7,6},{9,8},{10,9},{11,10},{12... | collective-permute-start | bytes 18440 | tf_op jit(solution)/shard_map/ppermute | solution.py:23
  340.2 6.1 %collective-permute-start.62 = (bf16[64,6,1,8]{0,3,2,1:T(8,128)(2,1)S(1)}, bf16[64,6,1,8]{0,3,2,1:T(8,128)(2,1)S(1)}, u32[]{:S(2)}, u32[]{:S(2)}) collective-permute-start(bf16[64,6,1,8]{0,3,2,1:T(8,128)(2,1)S(1)} %get-tuple-element.225), channel_id=1, source_target_pairs={{0,1},{1,2},{2,3},{3,4},{4,5},{5,6},{6,7},{8,9},{9,10},{10,11},{11... | collective-permute-start | bytes 18440 | tf_op jit(solution)/shard_map/ppermute | solution.py:21
  369.3 154.6 %all-reduce.7.cloned.1.call-start = ((), (), s32[]{:S(2)}) async-start(), calls=%async_computation | async-start | bytes 1769472 | tf_op jit(solution)/shard_map/psum | solution.py:266
  371.4 185.7 %all-reduce.13.cloned.1.call-start = ((), (), s32[]{:S(2)}) async-start(), calls=%async_computation.3 | async-start | bytes 253952 | tf_op jit(solution)/shard_map/psum | solution.py:266
  371.6 8.5 %collective-permute-start.23 = (f32[5,10,3,8]{3,2,1,0:T(4,128)S(1)}, f32[5,10,3,8]{3,2,1,0:T(4,128)S(1)}, u32[]{:S(2)}, u32[]{:S(2)}) collective-permute-start(f32[5,10,3,8]{3,2,1,0:T(4,128)S(1)} %get-tuple-element.141), channel_id=1, source_target_pairs={{0,1},{1,2},{2,3},{3,4},{4,5},{5,6},{6,7},{8,9},{9,10},{10,11},{11... | collective-permute-start | bytes 14408 | tf_op jit(solution)/shard_map/ppermute | solution.py:21
  376.5 8.4 %collective-permute-start.22 = (f32[5,10,3,8]{3,2,1,0:T(4,128)S(1)}, f32[5,10,3,8]{3,2,1,0:T(4,128)S(1)}, u32[]{:S(2)}, u32[]{:S(2)}) collective-permute-start(f32[5,10,3,8]{3,2,1,0:T(4,128)S(1)} %get-tuple-element.140), channel_id=1, source_target_pairs={{1,0},{2,1},{3,2},{4,3},{5,4},{6,5},{7,6},{9,8},{10,9},{11,10},{12... | collective-permute-start | bytes 14408 | tf_op jit(solution)/shard_map/ppermute | solution.py:23
  444.5 150.6 %all-reduce.9.cloned.1.call-start = ((), (), s32[]{:S(2)}) async-start(), calls=%async_computation.1 | async-start | bytes 1769472 | tf_op jit(solution)/shard_map/psum | solution.py:266
  (110 other events, 232.2 us)
Sparse Core Ops, SparseCore 0:
  369.4 75.0 all-reduce.10
  447.9 75.9 all-reduce.6
  526.2 30.8 all-reduce.12
  559.4 35.6 all-reduce.8
